TPU v7x, 512 devices: a whole 4x8x8 slice. The times are simulated.
512 devices in a mesh: dp: 32 (over y, x), seq: 16 (over z, core).
Axes of the slice: x: 4, y: 8, z: 8, core: 2. Of those that a mesh axis runs over, the one named last changes fastest.
Arguments:
- queries: bfloat16 [32, 2048, 2048], P('dp', 'seq'), may hold values from -6 to 6
- keys_in: bfloat16 [32, 2048, 2048], P('dp', 'seq'), may hold values from -6 to 6
- values_in: bfloat16 [32, 2048, 2048], P('dp', 'seq'), may hold values from -6 to 6
- grad_out: bfloat16 [32, 2048, 2048], P('dp', 'seq'), may hold values from -6 to 6
- feat_w: bfloat16 [2, 16, 128, 128], replicated, may hold values from -0.5 to 0.5
Outputs:
- grad_queries: bfloat16 [32, 2048, 2048], P('dp', 'seq')
- grad_keys: bfloat16 [32, 2048, 2048], P('dp', 'seq')
- grad_values: bfloat16 [32, 2048, 2048], P('dp', 'seq')
- grad_feat: float32 [4096, 128], P('dp')
All inputs are finite; a program needn't handle non-finite values.
Results may differ from a plain program's by a relative error of at most 0.0064.
Values sent between devices are 32-bit elements; how exact they have to be, the bound alone decides.
A program may use at most 128 MiB of HBM per device.

v0:
```python
import math
import jax
import jax.numpy as jnp
from jax import lax
from jax.sharding import PartitionSpec as P


def carried_in(value, axis, join, neutral, backward):
    count, mine = (lax.axis_size(axis), lax.axis_index(axis))
    pieces = lax.all_gather(value, axis)
    if backward:
        pieces = pieces[::-1]
        mine = count - 1 - mine
    running = jnp.full_like(value, 0) + jnp.asarray(neutral, value.dtype)

    def lap(position, running):
        longer = join(running, pieces[position])
        return jnp.where(position < mine, longer, running)

    return lax.fori_loop(0, count - 1, lap, running)


def add_one(earlier, later):
    return earlier + later


def body(queries, keys_in, values_in, grad_out, feat_w):
    seq_count = lax.axis_size("seq")
    rep_count = lax.axis_size("dp")
    rows = queries.shape[1]
    heads = feat_w.shape[1]
    hsize = feat_w.shape[2]
    scale = 1.0 / math.sqrt(hsize * rows * seq_count)
    gscale = 1.0 / math.sqrt(rows * seq_count * rep_count)
    shape = (rows, heads, hsize)
    q_heads = queries[0].reshape(shape)
    k_heads = keys_in[0].reshape(shape)
    v_heads = values_in[0].reshape(shape)
    g_heads = grad_out[0].reshape(shape)
    f32 = jnp.float32
    bf16 = jnp.bfloat16
    feat_q = jnp.einsum("tha,hab->thb", q_heads, feat_w[0], preferred_element_type=f32).astype(bf16)
    feat_k = jnp.einsum("tha,hab->thb", k_heads, feat_w[1], preferred_element_type=f32).astype(bf16)
    sterm = jnp.einsum("tha,thb->hab", feat_k, v_heads, preferred_element_type=f32)
    gterm = jnp.einsum("tha,thb->hab", feat_q, g_heads, preferred_element_type=f32)
    zeros = jnp.zeros(sterm.shape, f32)
    prefix = carried_in(sterm, "seq", add_one, zeros, False)
    suffix = carried_in(gterm, "seq", add_one, zeros, True)
    causal = jnp.tril(jnp.ones((rows, rows), dtype=bool))
    p_mat = jnp.where(
        causal, scale * jnp.einsum("tha,sha->hts", feat_q, feat_k, preferred_element_type=f32), 0.0
    ).astype(bf16)
    q_mat = jnp.where(
        causal,
        scale * jnp.einsum("tha,sha->hts", g_heads, v_heads, preferred_element_type=f32),
        0.0,
    ).astype(bf16)
    state_b = prefix.astype(bf16)
    grad_b = suffix.astype(bf16)
    d_featq = (
        scale * jnp.einsum("thb,hab->tha", g_heads, state_b, preferred_element_type=f32)
        + jnp.einsum("hts,sha->tha", q_mat, feat_k, preferred_element_type=f32)
    ).astype(bf16)
    d_featk = (
        scale * jnp.einsum("thb,hab->tha", v_heads, grad_b, preferred_element_type=f32)
        + jnp.einsum("hts,tha->sha", q_mat, feat_q, preferred_element_type=f32)
    ).astype(bf16)
    d_values = (
        scale * jnp.einsum("tha,hab->thb", feat_k, grad_b, preferred_element_type=f32)
        + jnp.einsum("hts,thb->shb", p_mat, g_heads, preferred_element_type=f32)
    ).astype(bf16)
    d_queries = jnp.einsum("thb,hab->tha", d_featq, feat_w[0], preferred_element_type=f32).astype(
        bf16
    )
    d_keys = jnp.einsum("thb,hab->tha", d_featk, feat_w[1], preferred_element_type=f32).astype(bf16)
    wgrad_q = jnp.einsum("tha,thb->hab", q_heads, d_featq, preferred_element_type=f32)
    wgrad_k = jnp.einsum("tha,thb->hab", k_heads, d_featk, preferred_element_type=f32)
    local_grad = jnp.stack([wgrad_q, wgrad_k]).reshape(2 * heads * hsize, hsize)
    seq_total = lax.psum(local_grad, "seq")
    owned = lax.psum_scatter(seq_total, "dp", scatter_dimension=0, tiled=True)
    flat = (1, rows, heads * hsize)
    return (d_queries.reshape(flat), d_keys.reshape(flat), d_values.reshape(flat), owned * gscale)


def solution(mesh):
    return jax.shard_map(
        body,
        mesh=mesh,
        in_specs=(
            P("dp", "seq", None),
            P("dp", "seq", None),
            P("dp", "seq", None),
            P("dp", "seq", None),
            P(),
        ),
        out_specs=(P("dp", "seq", None), P("dp", "seq", None), P("dp", "seq", None), P("dp", None)),
        check_vma=False,
    )
```

profile of v0, /device:TPU:1, one launch (start us, length us, event | category | flops | bytes accessed | tf_op | source)
XLA Modules:
  0.0 593.4 jit_solution(17331871863249463423)
XLA Ops:
  18.7 2.4 fusion.5
  21.1 96.6 %all-gather.5.cloned.1.call-done = f32[256,128,128]{2,1,0:T(8,128)} async-done(((f32[16,128,128]{2,1,0:T(8,128)}), f32[256,128,128]{2,1,0:T(8,128)}) %all-gather.5.cloned.1.call-update) | async-done | bytes 16777232 | tf_op jit(solution)/shard_map/all_gather | solution.py:10
  117.7 24.4 %while.28 = (s32[]{:T(128)}, f32[16,128,128]{2,1,0:T(8,128)S(1)}, s32[]{:T(128)}, f32[16,16,128,128]{3,2,1,0:T(8,128)}, s32[]{:T(128)}, /*index=5*/s32[]{:T(128)}) while((s32[]{:T(128)}, f32[16,128,128]{2,1,0:T(8,128)S(1)}, s32[]{:T(128)}, f32[16,16,128,128]{3,2,1,0:T(8,128)}, s32[]{:T(128)}, /*index=5*/s32[]{:T(128)}) %tuple.79), condition=%wide.region_1.2_spmd.clone, body=%wide.region_0.1_spmd.clone.sunk | while | flops 786436 | bytes 3145821 | solution.py:20
  119.3 1.6 add_select_fusion.4
  122.6 1.6 add_select_fusion.4
  125.8 1.6 add_select_fusion.4
  129.0 1.6 add_select_fusion.4
  130.6 1.7 add_select_fusion.4
  134.0 1.6 add_select_fusion.4
  137.2 1.6 add_select_fusion.4
  138.8 1.7 add_select_fusion.4
  140.5 1.6 add_select_fusion.4
  144.0 2.5 convolution_bitcast_fusion.2
  146.5 70.1 %all-gather.7.cloned.1.call-done = f32[256,128,128]{2,1,0:T(8,128)} async-done(((f32[16,128,128]{2,1,0:T(8,128)}), f32[256,128,128]{2,1,0:T(8,128)}) %all-gather.7.cloned.1.call-update) | async-done | bytes 16777232 | tf_op jit(solution)/shard_map/all_gather | solution.py:10
  216.6 11.6 %rev.3 = f32[16,16,128,128]{3,2,1,0:T(8,128)} reverse(f32[16,16,128,128]{3,2,1,0:T(8,128)} %bitcast.81), dimensions={0} | reverse | bytes 33554432 | tf_op jit(solution)/shard_map/rev | solution.py:12
  228.3 24.2 %while.29 = (s32[]{:T(128)}, f32[16,128,128]{2,1,0:T(8,128)S(1)}, s32[]{:T(128)}, f32[16,16,128,128]{3,2,1,0:T(8,128)}, s32[]{:T(128)}, /*index=5*/s32[]{:T(128)}) while((s32[]{:T(128)}, f32[16,128,128]{2,1,0:T(8,128)S(1)}, s32[]{:T(128)}, f32[16,16,128,128]{3,2,1,0:T(8,128)}, s32[]{:T(128)}, /*index=5*/s32[]{:T(128)}) %tuple.68), condition=%wide.region_3.4_spmd.clone, body=%wide.region_2.3_spmd.clone.sunk | while | flops 786436 | bytes 3145821 | solution.py:20
  228.3 1.6 add_select_fusion.5
  229.9 1.6 add_select_fusion.5
  257.7 2.8 pad_maximum_fusion
  260.6 2.1 convolution_convert_fusion.1
  264.0 1.7 fusion.8
  265.7 208.6 %reduce-scatter.2.cloned.1.call-done = f32[128,128]{1,0:T(8,128)} async-done(((f32[4096,128]{1,0:T(8,128)}), f32[128,128]{1,0:T(8,128)}) %reduce-scatter.2.cloned.1.call-update) | async-done | bytes 65552 | tf_op jit(solution)/shard_map/reduce_scatter | solution.py:80
  476.9 2.0 copy.52
  479.9 105.5 %all-reduce.2.cloned.1.call-done = f32[128,128]{1,0:T(8,128)} async-done(((f32[128,128]{1,0:T(8,128)}), f32[128,128]{1,0:T(8,128)}) %all-reduce.2.cloned.1.call-update) | async-done | bytes 65552 | tf_op jit(solution)/shard_map/psum | solution.py:79
  (60 shorter events, 55.0 us)
Async XLA Ops:
  7.2 110.5 %all-gather.5.cloned.1.call-start = ((), (), s32[]{:S(2)}) async-start(), calls=%async_computation.1 | async-start | bytes 17825792 | tf_op jit(solution)/shard_map/all_gather | solution.py:10
  8.5 4.3 copy-start.3
  9.9 5.6 copy-start.4
  12.8 203.8 %all-gather.7.cloned.1.call-start = ((), (), s32[]{:S(2)}) async-start(), calls=%async_computation.2 | async-start | bytes 17825792 | tf_op jit(solution)/shard_map/all_gather | solution.py:10
  15.5 3.2 copy-start.5
  17.1 1.6 copy-start
  18.6 455.7 %reduce-scatter.2.cloned.1.call-start = ((), (), s32[]{:S(2)}) async-start(), calls=%async_computation.3 | async-start | bytes 2162688 | tf_op jit(solution)/shard_map/reduce_scatter | solution.py:80
  228.3 25.8 %copy-start.1 = (bf16[128,16,128]{0,2,1:T(8,128)(2,1)S(1)}, bf16[128,16,128]{0,2,1:T(8,128)(2,1)}, u32[]{:S(2)}) copy-start(bf16[128,16,128]{0,2,1:T(8,128)(2,1)} %copy-done) | copy-start | bytes 1572868
  255.4 0.8 copy-start.2
  260.5 324.9 %all-reduce.2.cloned.1.call-start = ((), (), s32[]{:S(2)}) async-start(), calls=%async_computation.4 | async-start | bytes 131072 | tf_op jit(solution)/shard_map/psum | solution.py:79
Sparse Core Ops, SparseCore 0:
  12.9 104.7 all-gather.4
  119.8 96.7 all-gather.6
  260.6 213.6 reduce-scatter.1
  476.6 108.7 all-reduce.1
where the time goes:
time: 595 us; the launch traced here: 593 us
  waiting for transfers between devices  481 us (81%)
  other arithmetic  52.2 us (9%)
  matrix products  23.7 us (4%)
  local copies, waits for them, and re-layouts  21.8 us (4%)
  between operations  14 us (2%)
    reduce_scatter x1, waiting for transfers between devices, body(): owned = lax.psum_scatter(seq_total, 'dp', scatter_dimension=0, tiled=True)  209 us
    all_gather x2, waiting for transfers between devices, carried_in(): pieces = lax.all_gather(value, axis)  167 us
    psum x1, waiting for transfers between devices, body(): seq_total = lax.psum(local_grad, 'seq')  105 us
    select_n x30, other arithmetic, lap(): return jnp.where(position < mine, longer, running)  48 us
  transfers between devices with their start and end apart: 4, of which 4 were waited for; matrix products, arithmetic and copies ran while one was open for 8% of the time, Pallas kernels for 0%

commit v1 on v0

--- a/solution.py
+++ b/solution.py
@@ -3,6 +3,16 @@
 import jax.numpy as jnp
 from jax import lax
 from jax.sharding import PartitionSpec as P
+from jax.lax import axis_size, ppermute
+
+
+def deliver_ratios(mine_x):
+    axis_id = "seq"
+    low = mine_x
+    ndev = axis_size(axis_id)
+    for k in [dev_j for dev_j in (1, 2, 4, 8, 16) if dev_j < ndev]:
+        low = low + ppermute(low, axis_id, list(map(lambda jj: (jj, jj ^ k), range(ndev))))
+    return low
 
 
 def carried_in(value, axis, join, neutral, backward):
@@ -76,7 +86,7 @@
     wgrad_q = jnp.einsum("tha,thb->hab", q_heads, d_featq, preferred_element_type=f32)
     wgrad_k = jnp.einsum("tha,thb->hab", k_heads, d_featk, preferred_element_type=f32)
     local_grad = jnp.stack([wgrad_q, wgrad_k]).reshape(2 * heads * hsize, hsize)
-    seq_total = lax.psum(local_grad, "seq")
+    seq_total = deliver_ratios(local_grad)
     owned = lax.psum_scatter(seq_total, "dp", scatter_dimension=0, tiled=True)
     flat = (1, rows, heads * hsize)
     return (d_queries.reshape(flat), d_keys.reshape(flat), d_values.reshape(flat), owned * gscale)

time: 595 us -> 733 us (1.23)
  waiting for transfers between devices: 481 us -> 614 us
  starting transfers between devices: 0.16 us -> 10.9 us
  matrix products: 23.7 us -> 15 us
    ppermute x0 -> x4, waiting for transfers between devices: none -> 236 us  [deliver_ratios(): ppermute(low, axis_id, list(map(lambda jj: (jj, jj ^ k), range(ndev))))]
    psum x1 -> x0, waiting for transfers between devices: 105 us -> none  [body(): seq_total = lax.psum(local_grad, 'seq')]
    ppermute x0 -> x4, starting transfers between devices: none -> 10.8 us  [deliver_ratios(): ppermute(low, axis_id, list(map(lambda jj: (jj, jj ^ k), range(ndev))))]
  transfers between devices with their start and end apart: 4 -> 7, of which waited for: 4 -> 7; matrix products, arithmetic and copies ran while one was open for 8% -> 5% of each run, Pallas kernels for 0% -> 0%
where the time goes in v1:
time: 733 us; the launch traced here: 728 us
  waiting for transfers between devices  614 us (84%)
  other arithmetic  51.8 us (7%)
  local copies, waits for them, and re-layouts  21.8 us (3%)
  matrix products  15 us (2%)
  between operations  14.1 us (2%)
  starting transfers between devices  10.9 us (1%)
    ppermute x4, waiting for transfers between devices, deliver_ratios(): ppermute(low, axis_id, list(map(lambda jj: (jj, jj ^ k), range(ndev))))  236 us
    reduce_scatter x1, waiting for transfers between devices, body(): owned = lax.psum_scatter(seq_total, 'dp', scatter_dimension=0, tiled=True)  207 us
    all_gather x2, waiting for transfers between devices, carried_in(): pieces = lax.all_gather(value, axis)  171 us
    select_n x30, other arithmetic, lap(): return jnp.where(position < mine, longer, running)  47.9 us
  transfers between devices with their start and end apart: 7, of which 7 were waited for; matrix products, arithmetic and copies ran while one was open for 5% of the time, Pallas kernels for 0%

profile of v1, /device:TPU:1, one launch (start us, length us, event | category | flops | bytes accessed | tf_op | source)
XLA Modules:
  0.0 727.8 jit_solution(15631212101687845351)
XLA Ops:
  15.5 2.4 fusion.5
  17.8 99.2 %all-gather.5.cloned.1.call-done = f32[256,128,128]{2,1,0:T(8,128)} async-done(((f32[16,128,128]{2,1,0:T(8,128)}), f32[256,128,128]{2,1,0:T(8,128)}) %all-gather.5.cloned.1.call-update) | async-done | bytes 16777232 | tf_op jit(solution)/shard_map/all_gather | solution.py:20
  117.0 24.4 %while.28 = (s32[]{:T(128)}, f32[16,128,128]{2,1,0:T(8,128)S(1)}, s32[]{:T(128)}, f32[16,16,128,128]{3,2,1,0:T(8,128)}, s32[]{:T(128)}, /*index=5*/s32[]{:T(128)}) while((s32[]{:T(128)}, f32[16,128,128]{2,1,0:T(8,128)S(1)}, s32[]{:T(128)}, f32[16,16,128,128]{3,2,1,0:T(8,128)}, s32[]{:T(128)}, /*index=5*/s32[]{:T(128)}) %tuple.77), condition=%wide.region_1.2_spmd.clone, body=%wide.region_0.1_spmd.clone.sunk | while | flops 786436 | bytes 3145821 | solution.py:30
  118.6 1.6 add_select_fusion.4
  121.8 1.6 add_select_fusion.4
  123.4 1.6 add_select_fusion.4
  125.1 1.6 add_select_fusion.4
  129.9 1.7 add_select_fusion.4
  138.1 1.7 add_select_fusion.4
  144.4 71.5 %all-gather.7.cloned.1.call-done = f32[256,128,128]{2,1,0:T(8,128)} async-done(((f32[16,128,128]{2,1,0:T(8,128)}), f32[256,128,128]{2,1,0:T(8,128)}) %all-gather.7.cloned.1.call-update) | async-done | bytes 16777232 | tf_op jit(solution)/shard_map/all_gather | solution.py:20
  215.9 11.6 %rev.3 = f32[16,16,128,128]{3,2,1,0:T(8,128)} reverse(f32[16,16,128,128]{3,2,1,0:T(8,128)} %bitcast.82), dimensions={0} | reverse | bytes 33554432 | tf_op jit(solution)/shard_map/rev | solution.py:22
  227.6 24.2 %while.29 = (s32[]{:T(128)}, f32[16,128,128]{2,1,0:T(8,128)S(1)}, s32[]{:T(128)}, f32[16,16,128,128]{3,2,1,0:T(8,128)}, s32[]{:T(128)}, /*index=5*/s32[]{:T(128)}) while((s32[]{:T(128)}, f32[16,128,128]{2,1,0:T(8,128)S(1)}, s32[]{:T(128)}, f32[16,16,128,128]{3,2,1,0:T(8,128)}, s32[]{:T(128)}, /*index=5*/s32[]{:T(128)}) %tuple.68), condition=%wide.region_3.4_spmd.clone, body=%wide.region_2.3_spmd.clone.sunk | while | flops 786436 | bytes 3145821 | solution.py:30
  251.8 1.6 convolution_multiply_fusion.2
  255.3 2.2 collective-permute-start
  257.4 3.9 collective-permute-done
  261.5 1.9 collective-permute-start.1
  263.5 46.9 %collective-permute-done.1 = f32[4096,128]{1,0:T(8,128)S(1)} collective-permute-done((f32[4096,128]{1,0:T(8,128)S(1)}, f32[4096,128]{1,0:T(8,128)S(1)}, u32[]{:S(2)}, u32[]{:S(2)}) %collective-permute-start.1) | collective-permute-done | bytes 2097184 | tf_op jit(solution)/shard_map/ppermute | solution.py:14
  310.6 3.3 collective-permute-start.2
  313.9 91.9 %collective-permute-done.2 = f32[4096,128]{1,0:T(8,128)S(1)} collective-permute-done((f32[4096,128]{1,0:T(8,128)S(1)}, f32[4096,128]{1,0:T(8,128)S(1)}, u32[]{:S(2)}, u32[]{:S(2)}) %collective-permute-start.2) | collective-permute-done | bytes 2097184 | tf_op jit(solution)/shard_map/ppermute | solution.py:14
  406.1 3.4 collective-permute-start.3
  409.5 93.6 %collective-permute-done.3 = f32[4096,128]{1,0:T(8,128)S(1)} collective-permute-done((f32[4096,128]{1,0:T(8,128)S(1)}, f32[4096,128]{1,0:T(8,128)S(1)}, u32[]{:S(2)}, u32[]{:S(2)}) %collective-permute-start.3) | collective-permute-done | bytes 2097184 | tf_op jit(solution)/shard_map/ppermute | solution.py:14
  506.0 2.6 fusion.8
  508.6 2.1 copy.54
  513.3 206.5 %reduce-scatter.2.cloned.1.call-done = f32[128,128]{1,0:T(8,128)} async-done(((f32[4096,128]{1,0:T(8,128)}), f32[128,128]{1,0:T(8,128)}) %reduce-scatter.2.cloned.1.call-update) | async-done | bytes 65552 | tf_op jit(solution)/shard_map/reduce_scatter | solution.py:90
  (89 shorter events, 58.6 us)
Async XLA Ops:
  7.2 2.8 copy-start.9
  7.2 109.8 %all-gather.5.cloned.1.call-start = ((), (), s32[]{:S(2)}) async-start(), calls=%async_computation.2 | async-start | bytes 17825792 | tf_op jit(solution)/shard_map/all_gather | solution.py:20
  8.6 3.4 copy-start.4
  10.0 0.8 copy-start.6
  10.0 2.1 copy-start.14
  10.8 1.7 copy-start.15
  12.1 203.8 %all-gather.7.cloned.1.call-start = ((), (), s32[]{:S(2)}) async-start(), calls=%async_computation.3 | async-start | bytes 17825792 | tf_op jit(solution)/shard_map/all_gather | solution.py:20
  12.7 2.7 copy-start.7
  13.1 0.8 copy-start
  15.4 704.4 %reduce-scatter.2.cloned.1.call-start = ((), (), s32[]{:S(2)}) async-start(), calls=%async_computation.1 | async-start | bytes 2162688 | tf_op jit(solution)/shard_map/reduce_scatter | solution.py:90
  141.4 1.1 copy-start.12
  141.4 1.5 copy-start.8
  251.8 1.7 copy-start.1
  251.8 1.7 copy-start.13
  251.8 2.8 copy-start.5
  253.5 1.6 copy-start.11
  253.8 0.8 copy-start.2
  255.3 6.1 collective-permute-start
  261.5 48.9 %collective-permute-start.1 = (f32[4096,128]{1,0:T(8,128)S(1)}, f32[4096,128]{1,0:T(8,128)S(1)}, u32[]{:S(2)}, u32[]{:S(2)}) collective-permute-start(f32[4096,128]{1,0:T(8,128)S(1)} %bitcast_add_fusion), channel_id=1, source_target_pairs={{0,2},{1,3},{2,0},{3,1},{4,6},{5,7},{6,4},{7,5},{8,10},{9,11},{10,... | collective-permute-start | bytes 6291464 | tf_op jit(solution)/shard_map/ppermute | solution.py:14
  310.6 95.2 %collective-permute-start.2 = (f32[4096,128]{1,0:T(8,128)S(1)}, f32[4096,128]{1,0:T(8,128)S(1)}, u32[]{:S(2)}, u32[]{:S(2)}) collective-permute-start(f32[4096,128]{1,0:T(8,128)S(1)} %add.85), channel_id=1, source_target_pairs={{0,4},{1,5},{2,6},{3,7},{4,0},{5,1},{6,2},{7,3},{8,12},{9,13},{10,... | collective-permute-start | bytes 6291464 | tf_op jit(solution)/shard_map/ppermute | solution.py:14
  406.1 97.0 %collective-permute-start.3 = (f32[4096,128]{1,0:T(8,128)S(1)}, f32[4096,128]{1,0:T(8,128)S(1)}, u32[]{:S(2)}, u32[]{:S(2)}) collective-permute-start(f32[4096,128]{1,0:T(8,128)S(1)} %add.86), channel_id=1, source_target_pairs={{0,8},{1,9},{2,10},{3,11},{4,12},{5,13},{6,14},{7,15},{8,0},{9,1},... | collective-permute-start | bytes 6291464 | tf_op jit(solution)/shard_map/ppermute | solution.py:14
  506.0 4.7 copy-start.10
  508.6 3.4 copy-start.3
Sparse Core Ops, SparseCore 0:
  12.2 104.7 all-gather.4
  119.1 96.7 all-gather.6
  504.8 215.0 reduce-scatter.1
